TPU v7x, 256 devices: a whole 4x4x8 slice. The times are simulated.
256 devices in a mesh: group: 16 (over z_lo, y), fsdp: 16 (over x, z_hi, core).
Axes of the slice: x: 4, y: 4, z: 8 (z_hi: 2, z_lo: 4; z = z_hi * 4 + z_lo), core: 2. Of those that a mesh axis runs over, the one named last changes fastest.
Arguments:
- frames: bfloat16 [16, 8192, 1280], P('group', 'fsdp'), may hold values from -6 to 6
- cotangent: bfloat16 [16, 8192, 1280], P('group', 'fsdp'), may hold values from -12 to 12
- mix_partner: int32 [16, 64], P('group', 'fsdp'), may hold values from 0 to 3
- lengths: int32 [16, 64], P('group', 'fsdp'), may hold values from 32 to 128, as said below
- inner_params: bfloat16 [16, 1280, 2, 2560], P('group', 'fsdp'), may hold values from -6 to 6
- first_moment: float32 [16, 1280, 2, 2560], P('group', 'fsdp'), may hold values from -6 to 6
- second_moment: float32 [16, 1280, 2, 2560], P('group', 'fsdp'), may hold values from 0.25 to 4
- outer_params: float32 [1280, 2, 2560], P('fsdp'), may hold values from -6 to 6
- momentum: float32 [1280, 2, 2560], P('fsdp'), may hold values from -3 to 3
Outputs:
- new_moment: float32 [16, 1280, 2, 2560], P('group', 'fsdp')
- new_outer: float32 [1280, 2, 2560], P('fsdp')
- new_momentum: float32 [1280, 2, 2560], P('fsdp')
Inputs may be any that keep to these rules, and one draw needn't show every extreme that they name: `lengths`: in every replica at least one utterance has all 128 frames.
All inputs are finite; a program needn't handle non-finite values.
Results may differ from a plain program's by a relative error of at most 0.004.
Values may be sent and summed in bfloat16 or wider, within the bound.
A program may use at most 128 MiB of HBM per device.

v0:
```python
import jax
import jax.numpy as jnp
from jax import lax
from jax.sharding import PartitionSpec as P

beta_one = 0.9
beta_two = 0.98
inner_rate = 0.08
decay_rate = 0.01
adam_eps = 1e-06
outer_rate = 0.7
nesterov_mu = 0.9
norm_eps = 1e-05
mix_weight = 0.5
inv_root_two = 0.7071067811865476
inv_root_tau = 0.3989422804014327
correction_one = 1.0 - beta_one**500.0
correction_two = 1.0 - beta_two**500.0


def gelu_parts(values):
    cumulative = 0.5 * (1.0 + jax.scipy.special.erf(values * inv_root_two))
    density = jnp.exp(-0.5 * values * values) * inv_root_tau
    return (values * cumulative, cumulative + values * density)


def normalize(mixed_rows):
    centre = jnp.mean(mixed_rows, axis=-1, keepdims=True)
    shifted = mixed_rows - centre
    spread = jnp.mean(shifted * shifted, axis=-1, keepdims=True)
    return (shifted * lax.rsqrt(spread + norm_eps)).astype(jnp.bfloat16)


def add_rows(left_rows, portion):
    return jnp.dot(left_rows, portion, preferred_element_type=jnp.float32)


def per_device(
    frames,
    cotangent,
    mix_partner,
    lengths,
    inner_params,
    first_moment,
    second_moment,
    outer_params,
    momentum,
):
    frame_rows = frames.shape[1]
    model_width = frames.shape[2]
    utt_count = mix_partner.shape[1]
    crop_frames = frame_rows // utt_count
    hidden_width = inner_params.shape[3]
    blocks = frames[0].reshape(utt_count, crop_frames, model_width).astype(jnp.float32)
    partner_rows = jnp.take(blocks, mix_partner[0], axis=0)
    mixed_rows = blocks + mix_weight * partner_rows
    normed = normalize(mixed_rows).reshape(frame_rows, model_width)
    offsets = lax.broadcasted_iota(jnp.int32, (utt_count, crop_frames), 1)
    keep_mask = (offsets < lengths[0][:, None]).reshape(frame_rows, 1).astype(jnp.bfloat16)
    masked_grad = cotangent[0] * keep_mask
    pre_sum = add_rows(normed, lax.all_gather(inner_params[0, :, 0, :], "fsdp", axis=0, tiled=True))
    back_sum = add_rows(
        masked_grad, lax.all_gather(inner_params[0, :, 1, :], "fsdp", axis=0, tiled=True)
    )
    pre_act = pre_sum * model_width ** (-0.5)
    back_grad = back_sum * hidden_width ** (-0.5)
    activation, derivative = gelu_parts(pre_act)
    activation = activation.astype(jnp.bfloat16)
    hidden_grad = (back_grad * derivative).astype(jnp.bfloat16)
    grad_in = lax.dot_general(
        normed, hidden_grad, (((0,), (0,)), ((), ())), preferred_element_type=jnp.float32
    ) * model_width ** (-0.5)
    grad_out = lax.dot_general(
        masked_grad, activation, (((0,), (0,)), ((), ())), preferred_element_type=jnp.float32
    ) * hidden_width ** (-0.5)
    gradients = lax.psum_scatter(
        jnp.stack((grad_in, grad_out), axis=1).astype(jnp.bfloat16),
        "fsdp",
        scatter_dimension=0,
        tiled=True,
    ).astype(jnp.float32)
    new_moment = beta_one * first_moment[0] + (1.0 - beta_one) * gradients
    new_second = beta_two * second_moment[0] + (1.0 - beta_two) * gradients * gradients
    update = new_moment / correction_one / (jnp.sqrt(new_second / correction_two) + adam_eps)
    current = inner_params[0].astype(jnp.float32)
    stepped = current - inner_rate * (update + decay_rate * current)
    pseudo = outer_params - stepped
    replica_count = lax.axis_size("group")
    totals = lax.psum(pseudo, "group")
    average = totals * (1.0 / replica_count)
    new_momentum = nesterov_mu * momentum + average
    new_outer = outer_params - outer_rate * (average + nesterov_mu * new_momentum)
    return (new_moment[None], new_outer, new_momentum)


def solution(mesh):
    in_specs = (
        P("group", "fsdp", None),
        P("group", "fsdp", None),
        P("group", "fsdp"),
        P("group", "fsdp"),
        P("group", "fsdp", None, None),
        P("group", "fsdp", None, None),
        P("group", "fsdp", None, None),
        P("fsdp", None, None),
        P("fsdp", None, None),
    )
    out_specs = (P("group", "fsdp", None, None), P("fsdp", None, None), P("fsdp", None, None))
    return jax.shard_map(
        per_device, mesh=mesh, in_specs=in_specs, out_specs=out_specs, check_vma=False
    )
```

profile of v0, /device:TPU:2, one launch (start us, length us, event | category | flops | bytes accessed | tf_op | source)
XLA Modules:
  0.0 577.6 jit_solution(5133253302970498098)
XLA Ops:
  7.2 0.0 copy-start
  7.2 0.0 all-gather.7.cloned.1.call-start
  7.2 2.9 fusion.36
  10.1 0.8 copy.50
  10.9 0.0 all-gather.7.cloned.1.call-update
  10.9 0.0 all-gather.5.cloned.1.call-start
  11.0 0.0 copy-start.7
  11.0 0.8 copy.51
  11.8 0.0 all-gather.5.cloned.1.call-update
  11.8 0.0 reduce-scatter.2.cloned.1.call-start
  11.9 0.0 copy-done
  11.9 1.7 convert.32
  13.6 0.0 copy-done.7
  13.6 0.0 copy-start.8
  13.6 2.5 gather_fusion
  16.1 0.0 copy-start.1
  16.1 0.1 broadcast_bitcast_fusion
  16.2 0.0 copy-done.8
  16.2 0.1 fusion.33
  16.2 2.0 fusion.28
  18.2 0.0 copy-done.1
  18.2 0.8 multiply_reduce_fusion
  19.0 1.7 fusion.16
  20.8 87.6 %all-gather.7.cloned.1.call-done = bf16[1,1280,1,2560]{3,1,2,0:T(8,128)(2,1)} async-done(((bf16[1,80,1,2560]{3,1,2,0:T(8,128)(2,1)}), bf16[1,1280,1,2560]{3,1,2,0:T(8,128)(2,1)}) %all-gather.7.cloned.1.call-update) | async-done | bytes 6553616 | tf_op jit(solution)/shard_map/all_gather | solution.py:61
  108.4 6.1 %fusion.4 = f32[512,2560]{1,0:T(8,128)S(1)} fusion(bf16[512,1280]{1,0:T(8,128)(2,1)} %fusion.16, bf16[1,1280,1,2560]{3,1,2,0:T(8,128)(2,1)} %all-gather.7.cloned.1.call-done), kind=kOutput, calls=%fused_computation.8 | convolution fusion | flops 3355443200 | bytes 13107200 | tf_op jit(solution)/shard_map/dot_general | solution.py:35
  114.4 0.0 copy-start.9
  114.4 2.3 copy-done.9
  116.7 0.0 copy-done.6
  116.7 5.8 %fusion.2 = bf16[1280,1,2560]{2,0,1:T(8,128)(2,1)} fusion(f32[512,2560]{1,0:T(8,128)S(1)} %fusion.4, bf16[1,512,1280]{2,1,0:T(8,128)(2,1)S(1)} %copy-done.6, bf16[512]{0:T(512)(128)(2,1)S(1)} %fusion.33), kind=kOutput, calls=%fused_computation.6 | convolution fusion | flops 3370516480 | bytes 13108224 | tf_op jit(solution)/shard_map/dot_general | solution.py:73
  122.5 79.0 %all-gather.5.cloned.1.call-done = bf16[1,1280,1,2560]{3,1,2,0:T(8,128)(2,1)} async-done(((bf16[1,80,1,2560]{3,1,2,0:T(8,128)(2,1)}), bf16[1,1280,1,2560]{3,1,2,0:T(8,128)(2,1)}) %all-gather.5.cloned.1.call-update) | async-done | bytes 6553616 | tf_op jit(solution)/shard_map/all_gather | solution.py:63
  201.6 7.9 %multiply_convert_fusion.1 = bf16[512,2560]{1,0:T(8,128)(2,1)S(1)} fusion(f32[512,2560]{1,0:T(8,128)} %copy-done.9, bf16[1,1280,1,2560]{3,1,2,0:T(8,128)(2,1)} %all-gather.5.cloned.1.call-done, bf16[1,512,1280]{2,1,0:T(8,128)(2,1)S(1)} %copy-done.6, bf16[512]{0:T(512)(128)(2,1)S(1)} %fusion.33), kind=kOutput, calls=%fused_computation.13 | convolution fusion | flops 3371827200 | bytes 15729664 | tf_op jit(solution)/shard_map/dot_general | solution.py:35
  209.5 0.0 copy-done.5
  209.5 0.0 copy-start.3
  209.5 3.9 fusion.3
  213.4 0.0 copy-done.3
  213.4 5.6 pad_maximum_fusion
  219.0 0.0 reduce-scatter.2.cloned.1.call-update
  219.0 0.2 all-reduce.2.cloned.1.call-start
  219.2 176.1 %reduce-scatter.2.cloned.1.call-done = bf16[80,2,2560]{2,0,1:T(8,128)(2,1)} async-done(((bf16[1280,2,2560]{2,0,1:T(8,128)(2,1)}), bf16[80,2,2560]{2,0,1:T(8,128)(2,1)}) %reduce-scatter.2.cloned.1.call-update) | async-done | bytes 819216 | tf_op jit(solution)/shard_map/reduce_scatter | solution.py:76
  395.3 0.0 copy-done.2
  395.3 5.4 fusion.21
  400.7 0.0 all-reduce.2.cloned.1.call-update
  400.8 2.4 copy.29
  403.2 160.2 %all-reduce.2.cloned.1.call-done = f32[80,2,2560]{2,0,1:T(8,128)} async-done(((f32[80,2,2560]{2,0,1:T(8,128)}), f32[80,2,2560]{2,0,1:T(8,128)}) %all-reduce.2.cloned.1.call-update) | async-done | bytes 1638416 | tf_op jit(solution)/shard_map/psum | solution.py:89
  563.4 0.0 copy-done.4
  563.4 2.8 fusion.27
  566.2 2.4 copy.31
  568.6 2.4 copy.30
  (9 shorter events, 0.0 us)
Async XLA Ops:
  7.2 4.7 copy-start
  7.2 101.2 %all-gather.7.cloned.1.call-start = ((), (), s32[]{:S(2)}) async-start(), calls=%async_computation.4 | async-start | bytes 6963200 | tf_op jit(solution)/shard_map/all_gather | solution.py:61
  10.9 190.6 %all-gather.5.cloned.1.call-start = ((), (), s32[]{:S(2)}) async-start(), calls=%async_computation.3 | async-start | bytes 6963200 | tf_op jit(solution)/shard_map/all_gather | solution.py:63
  11.0 2.6 copy-start.7
  11.8 383.5 %reduce-scatter.2.cloned.1.call-start = ((), (), s32[]{:S(2)}) async-start(), calls=%async_computation.1 | async-start | bytes 13926400 | tf_op jit(solution)/shard_map/reduce_scatter | solution.py:76
  13.6 2.6 copy-start.8
  16.1 2.2 copy-start.1
  20.8 96.0 %copy-start.6 = (bf16[1,512,1280]{2,1,0:T(8,128)(2,1)S(1)}, bf16[1,512,1280]{2,1,0:T(8,128)(2,1)}, u32[]{:S(2)}) copy-start(bf16[1,512,1280]{2,1,0:T(8,128)(2,1)} %param.10) | copy-start | bytes 3932164
  114.4 2.3 copy-start.9
  122.5 87.0 %copy-start.5 = (bf16[512,1280]{1,0:T(8,128)(2,1)S(1)}, bf16[512,1280]{1,0:T(8,128)(2,1)}, u32[]{:S(2)}) copy-start(bf16[512,1280]{1,0:T(8,128)(2,1)} %fusion.16) | copy-start | bytes 3932164
  209.5 3.9 copy-start.3
  219.0 176.4 %copy-start.2 = (bf16[1,80,2,2560]{3,2,1,0:T(2,128)(2,1)S(1)}, bf16[1,80,2,2560]{3,2,1,0:T(2,128)(2,1)}, u32[]{:S(2)}) copy-start(bf16[1,80,2,2560]{3,2,1,0:T(2,128)(2,1)} %param.13) | copy-start | bytes 2457604
  219.0 344.4 %all-reduce.2.cloned.1.call-start = ((), (), s32[]{:S(2)}) async-start(), calls=%async_computation.2 | async-start | bytes 3276800 | tf_op jit(solution)/shard_map/psum | solution.py:89
  400.7 162.7 %copy-start.4 = (f32[80,2,2560]{2,1,0:T(2,128)S(1)}, f32[80,2,2560]{2,1,0:T(2,128)}, u32[]{:S(2)}) copy-start(f32[80,2,2560]{2,1,0:T(2,128)} %param.16) | copy-start | bytes 4915204
Sparse Core Ops, SparseCore 0:
  11.3 97.0 all-gather.6
  111.6 89.9 all-gather.4
  219.1 176.1 reduce-scatter.1
  400.9 162.4 all-reduce.1
where the time goes:
time: 578 us
  waiting for transfers between devices  503 us (87%)
  matrix products  23.7 us (4%)
  other arithmetic  20 us (3%)
  local copies, waits for them, and re-layouts  16.6 us (3%)
  between operations  13.9 us (2%)
    reduce_scatter x1, waiting for transfers between devices, per_device(): lax.psum_scatter(jnp.stack((grad_in, grad_out), axis=1).astype(jnp.bfloat...  176 us
    psum x1, waiting for transfers between devices, per_device(): totals = lax.psum(pseudo, 'group')  160 us
    all_gather x1, waiting for transfers between devices, per_device(): lax.all_gather(inner_params[0, :, 0, :], 'fsdp', axis=0, tiled=True)  87.6 us
    all_gather x1, waiting for transfers between devices, per_device(): lax.all_gather(inner_params[0, :, 1, :], 'fsdp', axis=0, tiled=True)  79 us
    dot_general x2, matrix products, add_rows(): return jnp.dot(left_rows, portion, preferred_element_type=jnp.float32)  14 us
  transfers between devices with their start and end apart: 4, of which 4 were waited for; matrix products, arithmetic and copies ran while one was open for 4% of the time, Pallas kernels for 0%

commit v1 on v0

--- a/solution.py
+++ b/solution.py
@@ -86,7 +86,7 @@
     stepped = current - inner_rate * (update + decay_rate * current)
     pseudo = outer_params - stepped
     replica_count = lax.axis_size("group")
-    totals = lax.psum(pseudo, "group")
+    totals = jnp.sum(lax.all_gather(pseudo, "group"), axis=0)
     average = totals * (1.0 / replica_count)
     new_momentum = nesterov_mu * momentum + average
     new_outer = outer_params - outer_rate * (average + nesterov_mu * new_momentum)

time: 578 us -> 704 us (1.22)
  waiting for transfers between devices: 503 us -> 619 us
  other arithmetic: 20 us -> 29.9 us
    all_gather x0 -> x1, waiting for transfers between devices: none -> 276 us  [per_device(): totals = jnp.sum(lax.all_gather(pseudo, 'group'), axis=0)]
    psum x1 -> x0, waiting for transfers between devices: 160 us -> none  [per_device(): totals = lax.psum(pseudo, 'group')]
    reduce_sum x0 -> x1, other arithmetic: none -> 10.3 us  [per_device(): totals = jnp.sum(lax.all_gather(pseudo, 'group'), axis=0)]
  transfers between devices with their start and end apart: 4 -> 4, of which waited for: 4 -> 4; matrix products, arithmetic and copies ran while one was open for 4% -> 3% of each run, Pallas kernels for 0% -> 0%
where the time goes in v1:
time: 704 us; the launch traced here: 703 us
  waiting for transfers between devices  619 us (88%)
  other arithmetic  29.9 us (4%)
  matrix products  23.7 us (3%)
  local copies, waits for them, and re-layouts  16.6 us (2%)
  between operations  13.9 us (2%)
    all_gather x1, waiting for transfers between devices, per_device(): totals = jnp.sum(lax.all_gather(pseudo, 'group'), axis=0)  276 us
    reduce_scatter x1, waiting for transfers between devices, per_device(): lax.psum_scatter(jnp.stack((grad_in, grad_out), axis=1).astype(jnp.bfloat...  176 us
    all_gather x1, waiting for transfers between devices, per_device(): lax.all_gather(inner_params[0, :, 0, :], 'fsdp', axis=0, tiled=True)  87.6 us
    all_gather x1, waiting for transfers between devices, per_device(): lax.all_gather(inner_params[0, :, 1, :], 'fsdp', axis=0, tiled=True)  79 us
  transfers between devices with their start and end apart: 4, of which 4 were waited for; matrix products, arithmetic and copies ran while one was open for 3% of the time, Pallas kernels for 0%

profile of v1, /device:TPU:2, one launch (start us, length us, event | category | flops | bytes accessed | tf_op | source)
XLA Modules:
  0.0 703.1 jit_solution(8073243558836537714)
XLA Ops:
  7.2 0.0 copy-start
  7.2 0.0 all-gather.9.cloned.1.call-start
  7.2 2.9 fusion.36
  10.1 0.8 copy.53
  10.9 0.0 all-gather.9.cloned.1.call-update
  10.9 0.0 all-gather.7.cloned.1.call-start
  11.0 0.0 copy-start.7
  11.0 0.8 copy.54
  11.8 0.0 all-gather.7.cloned.1.call-update
  11.8 0.0 reduce-scatter.2.cloned.1.call-start
  11.9 0.0 copy-done
  11.9 1.7 convert.32
  13.6 0.0 copy-done.7
  13.6 0.0 copy-start.8
  13.6 2.5 gather_fusion
  16.1 0.0 copy-start.1
  16.1 0.1 broadcast_bitcast_fusion
  16.2 0.0 copy-done.8
  16.2 0.1 fusion.33
  16.2 2.0 fusion.28
  18.2 0.0 copy-done.1
  18.2 0.8 multiply_reduce_fusion
  19.0 1.7 fusion.16
  20.8 87.6 %all-gather.9.cloned.1.call-done = bf16[1,1280,1,2560]{3,1,2,0:T(8,128)(2,1)} async-done(((bf16[1,80,1,2560]{3,1,2,0:T(8,128)(2,1)}), bf16[1,1280,1,2560]{3,1,2,0:T(8,128)(2,1)}) %all-gather.9.cloned.1.call-update) | async-done | bytes 6553616 | tf_op jit(solution)/shard_map/all_gather | solution.py:61
  108.4 6.1 fusion.4
  114.4 0.0 copy-start.9
  114.4 2.3 copy-done.9
  116.7 0.0 copy-done.6
  116.7 5.8 fusion.2
  122.5 79.0 %all-gather.7.cloned.1.call-done = bf16[1,1280,1,2560]{3,1,2,0:T(8,128)(2,1)} async-done(((bf16[1,80,1,2560]{3,1,2,0:T(8,128)(2,1)}), bf16[1,1280,1,2560]{3,1,2,0:T(8,128)(2,1)}) %all-gather.7.cloned.1.call-update) | async-done | bytes 6553616 | tf_op jit(solution)/shard_map/all_gather | solution.py:63
  201.6 7.9 %multiply_convert_fusion.1 = bf16[512,2560]{1,0:T(8,128)(2,1)S(1)} fusion(f32[512,2560]{1,0:T(8,128)} %copy-done.9, bf16[1,1280,1,2560]{3,1,2,0:T(8,128)(2,1)} %all-gather.7.cloned.1.call-done, bf16[1,512,1280]{2,1,0:T(8,128)(2,1)S(1)} %copy-done.6, bf16[512]{0:T(512)(128)(2,1)S(1)} %fusion.33), kind=kOutput, calls=%fused_computation.13 | convolution fusion | flops 3371827200 | bytes 15729664 | tf_op jit(solution)/shard_map/dot_general | solution.py:35
  209.5 0.0 copy-done.5
  209.5 0.0 copy-start.3
  209.5 3.9 fusion.3
  213.4 0.0 copy-done.3
  213.4 5.6 pad_maximum_fusion
  219.0 0.0 reduce-scatter.2.cloned.1.call-update
  219.0 0.2 all-gather.11.cloned.1.call-start
  219.2 176.1 %reduce-scatter.2.cloned.1.call-done = bf16[80,2,2560]{2,0,1:T(8,128)(2,1)} async-done(((bf16[1280,2,2560]{2,0,1:T(8,128)(2,1)}), bf16[80,2,2560]{2,0,1:T(8,128)(2,1)}) %reduce-scatter.2.cloned.1.call-update) | async-done | bytes 819216 | tf_op jit(solution)/shard_map/reduce_scatter | solution.py:76
  395.3 0.0 copy-done.2
  395.3 5.4 fusion.21
  400.7 0.0 all-gather.11.cloned.1.call-update
  400.8 2.4 copy.32
  403.2 275.9 %all-gather.11.cloned.1.call-done = f32[1280,2,2560]{2,0,1:T(8,128)} async-done(((f32[80,2,2560]{2,0,1:T(8,128)}), f32[1280,2,2560]{2,0,1:T(8,128)}) %all-gather.11.cloned.1.call-update) | async-done | bytes 26214416 | tf_op jit(solution)/shard_map/all_gather | solution.py:89
  679.1 10.3 %reduce_sum.29 = f32[80,2,2560]{2,0,1:T(8,128)S(1)} reduce(f32[16,80,2,2560]{3,1,0,2:T(8,128)} %bitcast.74, f32[]{:T(128)} %constant.29.clone.1), dimensions={0}, to_apply=%region_3.4 | reduce | flops 6144000 | bytes 27852804 | tf_op jit(solution)/shard_map/reduce_sum | solution.py:89
  689.4 2.3 fusion.27
  691.7 2.4 copy.34
  694.1 2.4 copy.33
  (10 shorter events, 0.0 us)
Async XLA Ops:
  7.2 4.7 copy-start
  7.2 101.2 %all-gather.9.cloned.1.call-start = ((), (), s32[]{:S(2)}) async-start(), calls=%async_computation.3 | async-start | bytes 6963200 | tf_op jit(solution)/shard_map/all_gather | solution.py:61
  10.9 190.6 %all-gather.7.cloned.1.call-start = ((), (), s32[]{:S(2)}) async-start(), calls=%async_computation.2 | async-start | bytes 6963200 | tf_op jit(solution)/shard_map/all_gather | solution.py:63
  11.0 2.6 copy-start.7
  11.8 383.5 %reduce-scatter.2.cloned.1.call-start = ((), (), s32[]{:S(2)}) async-start(), calls=%async_computation.1 | async-start | bytes 13926400 | tf_op jit(solution)/shard_map/reduce_scatter | solution.py:76
  13.6 2.6 copy-start.8
  16.1 2.2 copy-start.1
  20.8 96.0 %copy-start.6 = (bf16[1,512,1280]{2,1,0:T(8,128)(2,1)S(1)}, bf16[1,512,1280]{2,1,0:T(8,128)(2,1)}, u32[]{:S(2)}) copy-start(bf16[1,512,1280]{2,1,0:T(8,128)(2,1)} %param.10) | copy-start | bytes 3932164
  114.4 2.3 copy-start.9
  122.5 87.0 %copy-start.5 = (bf16[512,1280]{1,0:T(8,128)(2,1)S(1)}, bf16[512,1280]{1,0:T(8,128)(2,1)}, u32[]{:S(2)}) copy-start(bf16[512,1280]{1,0:T(8,128)(2,1)} %fusion.16) | copy-start | bytes 3932164
  209.5 3.9 copy-start.3
  219.0 176.4 %copy-start.2 = (bf16[1,80,2,2560]{3,2,1,0:T(2,128)(2,1)S(1)}, bf16[1,80,2,2560]{3,2,1,0:T(2,128)(2,1)}, u32[]{:S(2)}) copy-start(bf16[1,80,2,2560]{3,2,1,0:T(2,128)(2,1)} %param.13) | copy-start | bytes 2457604
  219.0 460.0 %all-gather.11.cloned.1.call-start = ((), (), s32[]{:S(2)}) async-start(), calls=%async_computation.4 | async-start | bytes 27852800 | tf_op jit(solution)/shard_map/all_gather | solution.py:89
  679.1 10.3 %copy-start.4 = (f32[80,2,2560]{2,1,0:T(2,128)S(1)}, f32[80,2,2560]{2,1,0:T(2,128)}, u32[]{:S(2)}) copy-start(f32[80,2,2560]{2,1,0:T(2,128)} %param.16) | copy-start | bytes 4915204
Sparse Core Ops, SparseCore 0:
  11.3 97.0 all-gather.8
  111.6 89.9 all-gather.6
  219.1 176.1 reduce-scatter.1
  400.9 278.1 all-gather.10
